TPU v7x, 128 devices: a whole 4x4x4 slice. The times are simulated.
128 devices in a mesh: axial: 4 (over x), azim: 32 (over z, y, core).
Axes of the slice: x: 4, y: 4, z: 4, core: 2. Of those that a mesh axis runs over, the one named last changes fastest.
Arguments:
- density: float32 [64, 256, 512], P(None, 'azim', 'axial'), may hold values from 0.5 to 2
- velocity: float32 [3, 64, 256, 512], P(None, None, 'azim', 'axial'), may hold values from -3 to 3
- pressure: float32 [64, 256, 512], P(None, 'azim', 'axial'), may hold values from 0.4 to 1.5
- axial_metric: float32 [3, 64, 256, 512], P(None, None, 'azim', 'axial'), may hold values from -4 to 4
- azim_metric: float32 [3, 64, 256, 512], P(None, None, 'azim', 'axial'), may hold values from -4 to 4
- volume: float32 [64, 256, 512], P(None, 'azim', 'axial'), may hold values from 0.5 to 2
- radial_term: float32 [5, 64, 256, 512], P(None, None, 'azim', 'axial'), may hold values from -6 to 6
- panel_area: float32 [256, 512], P('azim', 'axial'), may hold values from 0.5 to 2
- observer_ids: int32 [4, 256, 512], P(None, 'azim', 'axial'), may hold values from 0 to 511
- bin_ids: int32 [4, 256, 512], P(None, 'azim', 'axial'), may hold values from 0 to 127
- weight_ids: int32 [4, 256, 512], P(None, 'azim', 'axial'), may hold values from 0 to 255
- bin_weights: float32 [256], replicated, may hold values from 0.2 to 1
Outputs:
- new_state: float32 [5, 64, 256, 512], P(None, None, 'azim', 'axial')
- signals: float32 [512, 128], P(('axial', 'azim'))
All inputs are finite; a program needn't handle non-finite values.
Results may differ from a plain program's by a relative error of at most 0.0003.
Values sent between devices are 32-bit elements; how exact they have to be, the bound alone decides.
A program may use at most 128 MiB of HBM per device.

v0:
```python
import math
import jax
import jax.numpy as jnp
from jax import lax
from jax.sharding import PartitionSpec as P

OBSERVERS = 512
TIME_BINS = 128
GAMMA = 1.4
SECTION = 0.25
DERIV_ALPHA = 1.0 / 3.0
FILTER_ALPHA = 0.499
DERIV_A = 14.0 / 9.0
DERIV_B = 1.0 / 9.0
HIGHEST = lax.Precision.HIGHEST


def padded(cells, sides, width, closed):
    for axis, dim in sides:
        count = lax.axis_size(axis)
        ends = count if closed else count - 1
        head = lax.slice_in_dim(cells, 0, width, axis=dim)
        tail = lax.slice_in_dim(cells, cells.shape[dim] - width, cells.shape[dim], axis=dim)
        cells = jnp.concatenate(
            [
                lax.ppermute(tail, axis, [(i, (i + 1) % count) for i in range(ends)]),
                cells,
                lax.ppermute(head, axis, [((i + 1) % count, i) for i in range(ends)]),
            ],
            axis=dim,
        )
    return cells


def decay_root(alpha):
    return (-1.0 + math.sqrt(1.0 - 4.0 * alpha * alpha)) / (2.0 * alpha)


def signed_power(base, exponent):
    exponent = jnp.asarray(exponent)
    parity = jnp.where(exponent % 2 == 0, 1.0, -1.0)
    return parity * jnp.exp(exponent.astype(jnp.float32) * math.log(-base))


def deriv_side(extended, dim):
    length = extended.shape[dim] - 6

    def cells(offset):
        return lax.slice_in_dim(extended, 3 + offset, 3 + offset + length, axis=dim)

    return 0.5 * DERIV_A * (cells(1) - cells(-1)) + 0.25 * DERIV_B * (cells(2) - cells(-2))


def filter_side(extended, dim):
    length = extended.shape[dim] - 6

    def cells(offset):
        return lax.slice_in_dim(extended, 3 + offset, 3 + offset + length, axis=dim)

    beta = FILTER_ALPHA
    coeffs = [
        (11.0 + 10.0 * beta) / 16.0,
        (15.0 + 34.0 * beta) / 32.0,
        (-3.0 + 6.0 * beta) / 16.0,
        (1.0 - 2.0 * beta) / 32.0,
    ]
    total = coeffs[0] * cells(0)
    for shift in range(1, 4):
        total = total + 0.5 * coeffs[shift] * (cells(shift) + cells(-shift))
    return total


def fluxes(density, velocity, pressure, energy, metric, volume):
    contra = metric[0] * velocity[0] + metric[1] * velocity[1] + metric[2] * velocity[2]
    mass_flow = density * contra
    pieces = [volume * mass_flow]
    for comp in range(3):
        pieces.append(volume * (mass_flow * velocity[comp] + metric[comp] * pressure))
    pieces.append(volume * (energy + pressure) * contra)
    return jnp.stack(pieces)


def pad_axial(field):
    return padded(field, (("axial", 3),), 3, False)


def pad_azimuth(field):
    return padded(field, (("azim", 2),), 3, True)


def open_line(rhs, alpha):
    base = decay_root(alpha)
    factor_g = -alpha / base
    scale = 1.0 / (factor_g * (1.0 - base * base))
    width_here = rhs.shape[3]
    group_size = lax.axis_size("axial")
    device_pos = lax.axis_index("axial")
    total_len = width_here * group_size
    offsets = jnp.arange(width_here, dtype=jnp.int32)
    local_matrix = signed_power(base, jnp.abs(offsets[:, None] - offsets[None, :]))
    local_part = jnp.einsum("vraj,ij->vrai", rhs, local_matrix, precision=HIGHEST)
    first_moment = jnp.einsum(
        "vraj,j->vra", rhs, signed_power(base, width_here - 1 - offsets), precision=HIGHEST
    )
    last_moment = jnp.einsum("vraj,j->vra", rhs, signed_power(base, offsets), precision=HIGHEST)
    moments = jnp.stack([first_moment, last_moment])[None]
    piece = lax.all_gather(moments, "axial", axis=0, tiled=True)
    others = jnp.arange(piece.shape[0], dtype=jnp.int32)
    gap_up = device_pos - others
    w_left = jnp.where(
        gap_up > 0, signed_power(base, width_here * jnp.maximum(gap_up - 1, 0) + 1), 0.0
    )
    w_right = jnp.where(
        gap_up < 0, signed_power(base, width_here * jnp.maximum(-gap_up - 1, 0) + 1), 0.0
    )
    w_end = signed_power(base, width_here * (group_size - 1 - others))
    left_sum = jnp.einsum("k,kvra->vra", w_left, piece[:, 0], precision=HIGHEST)
    right_sum = jnp.einsum("k,kvra->vra", w_right, piece[:, 1], precision=HIGHEST)
    end_sum = jnp.einsum("k,kvra->vra", w_end, piece[:, 0], precision=HIGHEST)
    left_sum, right_sum, end_sum = (left_sum, right_sum, end_sum)
    position = device_pos * width_here + offsets
    result = local_part + signed_power(base, offsets) * left_sum[..., None]
    result = result + signed_power(base, width_here - 1 - offsets) * right_sum[..., None]
    result = result - signed_power(base, total_len + 1 - position) * end_sum[..., None]
    return scale * result


def cycle_line(rhs, alpha):
    base = decay_root(alpha)
    factor_g = -alpha / base
    width_here = rhs.shape[2]
    group_size = lax.axis_size("azim")
    device_pos = lax.axis_index("azim")
    total_len = width_here * group_size
    scale = 1.0 / (factor_g * (1.0 - base * base) * (1.0 - base**total_len))
    offsets = jnp.arange(width_here, dtype=jnp.int32)
    gap = jnp.abs(offsets[:, None] - offsets[None, :])
    local_matrix = scale * (signed_power(base, gap) + signed_power(base, total_len - gap))
    local_part = jnp.einsum("vrjx,ij->vrix", rhs, local_matrix, precision=HIGHEST)
    first_moment = jnp.einsum(
        "vrjx,j->vrx", rhs, signed_power(base, width_here - 1 - offsets), precision=HIGHEST
    )
    last_moment = jnp.einsum("vrjx,j->vrx", rhs, signed_power(base, offsets), precision=HIGHEST)
    moments = jnp.stack([first_moment, last_moment])[None]
    piece = lax.all_gather(moments, "azim", axis=0, tiled=True)
    others = jnp.arange(piece.shape[0], dtype=jnp.int32)
    shift = (device_pos - others) % group_size
    w_first = jnp.where(
        shift > 0, signed_power(base, width_here * jnp.maximum(shift - 1, 0) + 1), 0.0
    )
    w_last = jnp.where(
        shift > 0, signed_power(base, width_here * jnp.maximum(group_size - shift - 1, 0) + 1), 0.0
    )
    first_sum = jnp.einsum("k,kvrx->vrx", w_first, piece[:, 0], precision=HIGHEST)
    last_sum = jnp.einsum("k,kvrx->vrx", w_last, piece[:, 1], precision=HIGHEST)
    outer = signed_power(base, offsets)[:, None] * first_sum[:, :, None, :]
    outer = outer + signed_power(base, width_here - 1 - offsets)[:, None] * last_sum[:, :, None, :]
    return local_part + scale * outer


def per_device(
    density,
    velocity,
    pressure,
    axial_metric,
    azim_metric,
    volume,
    radial_term,
    panel_area,
    observer_ids,
    bin_ids,
    weight_ids,
    bin_weights,
):
    energy = pressure / (GAMMA - 1.0) + 0.5 * density * (
        velocity[0] ** 2 + velocity[1] ** 2 + velocity[2] ** 2
    )
    state = jnp.concatenate([density[None], density[None] * velocity, energy[None]], axis=0)
    axial_flux = fluxes(density, velocity, pressure, energy, axial_metric, volume)
    azim_flux = fluxes(density, velocity, pressure, energy, azim_metric, volume)
    axial_deriv = open_line(deriv_side(pad_axial(axial_flux), 3), DERIV_ALPHA)
    azim_deriv = cycle_line(deriv_side(pad_azimuth(azim_flux), 2), DERIV_ALPHA)
    sectioned = state + SECTION * (radial_term - (axial_deriv + azim_deriv) / volume)
    smoothed = open_line(filter_side(pad_axial(sectioned), 3), FILTER_ALPHA)
    new_state = cycle_line(filter_side(pad_azimuth(smoothed), 2), FILTER_ALPHA)
    surface = new_state[:, 0]
    source = panel_area * (surface[2] + surface[0] - 1.0)
    table_size = bin_weights.shape[0]
    one_hot = (
        weight_ids.reshape(-1)[:, None] == jnp.arange(table_size, dtype=jnp.int32)[None, :]
    ).astype(jnp.float32)
    entry_weight = jnp.dot(one_hot, bin_weights, precision=HIGHEST)
    values = entry_weight * jnp.broadcast_to(source[None], weight_ids.shape).reshape(-1)
    bucket = (observer_ids * TIME_BINS + bin_ids).reshape(-1)
    partial_signals = jax.ops.segment_sum(
        values, bucket, num_segments=OBSERVERS * TIME_BINS
    ).reshape(OBSERVERS, TIME_BINS)
    signals = lax.psum_scatter(partial_signals, ("axial", "azim"), scatter_dimension=0, tiled=True)
    return (new_state, signals)


def solution(mesh):
    placed = (
        P(None, "azim", "axial"),
        P(None, None, "azim", "axial"),
        P(None, "azim", "axial"),
        P(None, None, "azim", "axial"),
        P(None, None, "azim", "axial"),
        P(None, "azim", "axial"),
        P(None, None, "azim", "axial"),
        P("azim", "axial"),
        P(None, "azim", "axial"),
        P(None, "azim", "axial"),
        P(None, "azim", "axial"),
        P(),
    )
    return jax.shard_map(
        per_device,
        mesh=mesh,
        in_specs=placed,
        out_specs=(P(None, None, "azim", "axial"), P(("axial", "azim"), None)),
        check_vma=False,
    )
```

profile of v0, /device:TPU:1, one launch (start us, length us, event | category | flops | bytes accessed | tf_op | source)
XLA Modules:
  0.0 457.5 jit_solution(16983114548345051890)
XLA Ops:
  7.3 2.7 bitcast_dynamic-update-slice_fusion.4
  15.6 6.4 %collective-permute-done.2 = f32[5,64,3,128]{3,1,2,0:T(8,128)S(1)} collective-permute-done((f32[5,64,3,128]{3,1,2,0:T(8,128)S(1)}, f32[5,64,3,128]{3,1,2,0:T(8,128)S(1)}, u32[]{:S(2)}, u32[]{:S(2)}) %collective-permute-start.2) | collective-permute-done | bytes 491552 | tf_op jit(solution)/shard_map/ppermute | solution.py:28
  32.8 4.2 collective-permute-start.1
  42.7 5.7 %fusion.30 = f32[5,64,8,128]{3,2,1,0:T(8,128)S(1)} fusion(f32[5,64,8,3]{3,2,1,0:T(8,128)} %copy.17, f32[5,64,8,128]{3,2,1,0:T(8,128)S(1)} %bitcast_dynamic-update-slice_fusion.5, f32[5,64,8,3]{3,2,1,0:T(8,128)} %copy.15), kind=kLoop, calls=%fused_computation.64 | loop fusion | flops 2949120 | bytes 2682880 | tf_op jit(solution)/shard_map/add | solution.py:51
  48.3 17.3 %fusion.215 = f32[1,5,64,8]{3,0,2,1:T(1,128)S(1)} fusion(f32[5,64,8,128]{3,2,1,0:T(8,128)S(1)} %fusion.30), kind=kOutput, calls=%fused_computation.350 | convolution fusion | flops 3934336 | bytes 1320960 | tf_op jit(solution)/shard_map/vraj,j->vra/dot_general | solution.py:102
  65.7 17.7 %fusion.213 = f32[1,5,64,8]{3,0,2,1:T(1,128)S(1)} fusion(f32[5,64,8,128]{3,2,1,0:T(8,128)S(1)} %fusion.30), kind=kOutput, calls=%fused_computation.348 | convolution fusion | flops 3933568 | bytes 1320960 | tf_op jit(solution)/shard_map/vraj,j->vra/dot_general | solution.py:105
  83.5 9.9 %all-gather = f32[8,5,64,8]{2,3,1,0:T(8,128)S(1)} all-gather(f32[2,5,64,8]{2,3,1,0:T(8,128)S(1)} %pad_maximum_fusion.10), channel_id=2, replica_groups=mesh['axial'=4,'azim'=32] {'axial'}, dimensions={0}, use_global_device_ids=true | all-gather | bytes 102400 | tf_op jit(solution)/shard_map/all_gather | solution.py:107
  94.7 2.5 fusion.19
  97.3 5.2 %slice_bitcast_fusion.3 = (f32[32,5,64,128]{3,2,1,0:T(8,128)S(1)}, f32[32,5,64,128]{3,2,1,0:T(8,128)S(1)}) fusion(f32[32,2,5,64,128]{4,3,2,1,0:T(8,128)} %bitcast.355), kind=kLoop, calls=%fused_computation.4 | loop fusion | bytes 20971520 | tf_op jit(solution)/shard_map/squeeze | solution.py:154
  102.5 5.4 %fusion.6 = f32[1,5,64,128]{3,0,2,1:T(1,128)S(1)} fusion(f32[32,5,64,128]{3,2,1,0:T(8,128)S(1)} %get-tuple-element.12, s32[]{:T(128)S(6)} %axis_index.33), kind=kOutput, calls=%fused_computation.11 | convolution fusion | flops 15729728 | bytes 5406724 | tf_op jit(solution)/shard_map/k,kvrx->vrx/dot_general | solution.py:154
  108.0 5.6 %fusion.4 = f32[1,5,64,128]{3,0,2,1:T(1,128)S(1)} fusion(f32[32,5,64,128]{3,2,1,0:T(8,128)S(1)} %get-tuple-element.13, s32[]{:T(128)S(6)} %axis_index.33), kind=kOutput, calls=%fused_computation.9 | convolution fusion | flops 15729728 | bytes 5406724 | tf_op jit(solution)/shard_map/k,kvrx->vrx/dot_general | solution.py:155
  120.5 4.0 collective-permute-start.5
  127.7 6.2 %fusion.47 = f32[5,64,8,128]{3,2,1,0:T(8,128)S(1)} fusion(f32[5,64,8,3]{3,2,1,0:T(8,128)} %copy.25, f32[5,64,8,128]{3,2,1,0:T(8,128)S(1)} %fusion.21, f32[5,64,8,3]{3,2,1,0:T(8,128)} %copy.23), kind=kLoop, calls=%fused_computation.81 | loop fusion | flops 5242880 | bytes 2682880 | tf_op jit(solution)/shard_map/add | solution.py:69
  133.8 17.3 %fusion.204 = f32[1,5,64,8]{3,0,2,1:T(1,128)S(1)} fusion(f32[5,64,8,128]{3,2,1,0:T(8,128)S(1)} %fusion.47), kind=kOutput, calls=%fused_computation.339 | convolution fusion | flops 3934336 | bytes 1320960 | tf_op jit(solution)/shard_map/vraj,j->vra/dot_general | solution.py:102
  151.1 17.7 %fusion.202 = f32[1,5,64,8]{3,0,2,1:T(1,128)S(1)} fusion(f32[5,64,8,128]{3,2,1,0:T(8,128)S(1)} %fusion.47), kind=kOutput, calls=%fused_computation.337 | convolution fusion | flops 3933568 | bytes 1320960 | tf_op jit(solution)/shard_map/vraj,j->vra/dot_general | solution.py:105
  169.0 9.2 %all-gather.2 = f32[8,5,64,8]{2,3,1,0:T(8,128)S(1)} all-gather(f32[2,5,64,8]{2,3,1,0:T(8,128)S(1)} %pad_maximum_fusion.11), channel_id=4, replica_groups=mesh['axial'=4,'azim'=32] {'axial'}, dimensions={0}, use_global_device_ids=true | all-gather | bytes 102400 | tf_op jit(solution)/shard_map/all_gather | solution.py:107
  181.4 16.4 %collective-permute-start.6 = (f32[5,64,3,128]{3,1,2,0:T(8,128)S(1)}, f32[5,64,3,128]{3,1,2,0:T(8,128)S(1)}, u32[]{:S(2)}, u32[]{:S(2)}) collective-permute-start(f32[5,64,3,128]{3,1,2,0:T(8,128)S(1)} %copy.26), channel_id=1, source_target_pairs={{1,0},{2,1},{3,2},{4,3},{5,4},{6,5},{7,6},{8,7},{9,8},{10,9},{11,1... | collective-permute-start | bytes 1474568 | tf_op jit(solution)/shard_map/ppermute | solution.py:28
  199.6 4.1 collective-permute-done.7
  211.5 56.8 %all-gather.9.cloned.1.call-done = f32[64,5,64,128]{3,2,1,0:T(8,128)} async-done(((f32[2,5,64,128]{3,2,1,0:T(8,128)}), f32[64,5,64,128]{3,2,1,0:T(8,128)}) %all-gather.9.cloned.1.call-update) | async-done | bytes 10485776 | tf_op jit(solution)/shard_map/all_gather | solution.py:145
  268.3 5.2 %slice_bitcast_fusion.1 = (f32[32,5,64,128]{3,2,1,0:T(8,128)S(1)}, f32[32,5,64,128]{3,2,1,0:T(8,128)S(1)}) fusion(f32[32,2,5,64,128]{4,3,2,1,0:T(8,128)} %bitcast.356), kind=kLoop, calls=%fused_computation.2 | loop fusion | bytes 20971520 | tf_op jit(solution)/shard_map/squeeze | solution.py:154
  273.5 5.4 %fusion.2 = f32[1,5,64,128]{3,0,2,1:T(1,128)S(1)} fusion(f32[32,5,64,128]{3,2,1,0:T(8,128)S(1)} %get-tuple-element.10, s32[]{:T(128)S(6)} %axis_index.33), kind=kOutput, calls=%fused_computation.7 | convolution fusion | flops 15729728 | bytes 5406724 | tf_op jit(solution)/shard_map/k,kvrx->vrx/dot_general | solution.py:154
  278.9 5.6 %fusion = f32[1,5,64,128]{3,0,2,1:T(1,128)S(1)} fusion(f32[32,5,64,128]{3,2,1,0:T(8,128)S(1)} %get-tuple-element.11, s32[]{:T(128)S(6)} %axis_index.33), kind=kOutput, calls=%fused_computation.5 | convolution fusion | flops 15729728 | bytes 5406724 | tf_op jit(solution)/shard_map/k,kvrx->vrx/dot_general | solution.py:155
  286.0 22.6 %scatter_custom_fusion = f32[65536]{0:T(1024)} fusion(s32[4096]{0:T(1024)S(1)} %add_bitcast_fusion, f32[4096]{0:T(1024)S(1)} %bitcast_multiply_fusion.21, f32[]{:T(128)} %constant.254.clone.1), kind=kCustom, calls=%fused_computation.160 | custom fusion | flops 4096 | bytes 262148 | tf_op jit(solution)/shard_map/scatter-add | solution.py:195
  308.6 140.8 %all-reduce.3.cloned.1.call-done = f32[512,128]{1,0:T(8,128)} async-done(((f32[512,128]{1,0:T(8,128)}), f32[512,128]{1,0:T(8,128)}) %all-reduce.3.cloned.1.call-update) | async-done | bytes 262160
  (132 shorter events, 49.0 us)
Async XLA Ops:
  7.2 201.9 %copy-start = (f32[256]{0:T(256)S(1)}, f32[256]{0:T(256)}, u32[]{:S(2)}) copy-start(f32[256]{0:T(256)} %param.23) | copy-start | bytes 3076
  7.2 90.1 %all-gather.7.cloned.1.call-start = ((), (), s32[]{:S(2)}) async-start(), calls=%async_computation | async-start | bytes 10813440 | tf_op jit(solution)/shard_map/all_gather | solution.py:145
  12.4 14.7 %copy-start.12 = (f32[64,8,128]{2,1,0:T(8,128)}, f32[64,8,128]{2,1,0:T(8,128)S(1)}, u32[]{:S(2)}) copy-start(f32[64,8,128]{2,1,0:T(8,128)S(1)} %get-tuple-element.3) | copy-start | bytes 786436
  12.7 9.3 %collective-permute-start.2 = (f32[5,64,3,128]{3,1,2,0:T(8,128)S(1)}, f32[5,64,3,128]{3,1,2,0:T(8,128)S(1)}, u32[]{:S(2)}, u32[]{:S(2)}) collective-permute-start(f32[5,64,3,128]{3,1,2,0:T(8,128)S(1)} %copy.18), channel_id=1, source_target_pairs={{1,0},{2,1},{3,2},{4,3},{5,4},{6,5},{7,6},{8,7},{9,8},{10,9},{11,1... | collective-permute-start | bytes 1474568 | tf_op jit(solution)/shard_map/ppermute | solution.py:28
  14.2 8.1 %collective-permute-start.3 = (f32[5,64,3,128]{3,1,2,0:T(8,128)S(1)}, f32[5,64,3,128]{3,1,2,0:T(8,128)S(1)}, u32[]{:S(2)}, u32[]{:S(2)}) collective-permute-start(f32[5,64,3,128]{3,1,2,0:T(8,128)S(1)} %copy.20), channel_id=1, source_target_pairs={{0,1},{1,2},{2,3},{3,4},{4,5},{5,6},{6,7},{7,8},{8,9},{9,10},{10,1... | collective-permute-start | bytes 1474568 | tf_op jit(solution)/shard_map/ppermute | solution.py:26
  27.1 241.2 %all-gather.9.cloned.1.call-start = ((), (), s32[]{:S(2)}) async-start(), calls=%async_computation.1 | async-start | bytes 10813440 | tf_op jit(solution)/shard_map/all_gather | solution.py:145
  30.4 9.1 %collective-permute-start = (f32[5,64,8,3]{1,2,3,0:T(8,128)S(1)}, f32[5,64,8,3]{1,2,3,0:T(8,128)S(1)}, u32[]{:S(2)}, u32[]{:S(2)}) collective-permute-start(f32[5,64,8,3]{1,2,3,0:T(8,128)S(1)} %copy.14), channel_id=1, source_target_pairs={{32,0},{64,32},{96,64},{33,1},{65,33},{97,65},{34,2},{66,34},{98,6... | collective-permute-start | bytes 92168 | tf_op jit(solution)/shard_map/ppermute | solution.py:28
  32.8 8.3 %collective-permute-start.1 = (f32[5,64,8,3]{1,2,3,0:T(8,128)}, f32[5,64,8,3]{1,2,3,0:T(8,128)S(1)}, u32[]{:S(2)}, u32[]{:S(2)}) collective-permute-start(f32[5,64,8,3]{1,2,3,0:T(8,128)} %copy.16), channel_id=1, source_target_pairs={{0,32},{32,64},{64,96},{1,33},{33,65},{65,97},{2,34},{34,66},{66,9... | collective-permute-start | bytes 92168 | tf_op jit(solution)/shard_map/ppermute | solution.py:26
  102.5 11.1 %copy-start.22 = (f32[5,64,8,128]{3,2,1,0:T(8,128)S(1)}, f32[5,64,8,128]{3,2,1,0:T(8,128)}, u32[]{:S(2)}) copy-start(f32[5,64,8,128]{3,2,1,0:T(8,128)} %fusion.19) | copy-start | bytes 3932164
  107.9 5.7 %copy-start.3 = (f32[5,64,8,128]{3,2,1,0:T(8,128)S(1)}, f32[5,64,8,128]{3,2,1,0:T(8,128)}, u32[]{:S(2)}) copy-start(f32[5,64,8,128]{3,2,1,0:T(8,128)} %copy-done.2) | copy-start | bytes 3932164
  107.9 5.7 %copy-start.5 = (f32[64,8,128]{2,1,0:T(8,128)S(1)}, f32[64,8,128]{2,1,0:T(8,128)}, u32[]{:S(2)}) copy-start(f32[64,8,128]{2,1,0:T(8,128)} %param.17) | copy-start | bytes 786436
  107.9 5.7 %copy-start.10 = (f32[64,8,128]{2,1,0:T(8,128)S(1)}, f32[64,8,128]{2,1,0:T(8,128)}, u32[]{:S(2)}) copy-start(f32[64,8,128]{2,1,0:T(8,128)} %param.12) | copy-start | bytes 786436
  107.9 5.7 %copy-start.13 = (f32[64,8,128]{2,1,0:T(8,128)S(1)}, f32[64,8,128]{2,1,0:T(8,128)}, u32[]{:S(2)}) copy-start(f32[64,8,128]{2,1,0:T(8,128)} %copy-done.12) | copy-start | bytes 786436
  107.9 5.7 %copy-start.15 = (f32[3,64,8,128]{3,2,1,0:T(8,128)S(1)}, f32[3,64,8,128]{3,2,1,0:T(8,128)}, u32[]{:S(2)}) copy-start(f32[3,64,8,128]{3,2,1,0:T(8,128)} %broadcast_multiply_fusion.1) | copy-start | bytes 2359300
  108.0 5.7 %copy-start.19 = (f32[5,64,8,128]{3,2,1,0:T(8,128)S(1)}, f32[5,64,8,128]{3,2,1,0:T(8,128)}, u32[]{:S(2)}) copy-start(f32[5,64,8,128]{3,2,1,0:T(8,128)} %param.18) | copy-start | bytes 3932164
  108.0 5.7 %copy-start.21 = (f32[8]{0:T(128)S(1)}, f32[8]{0:T(128)}, u32[]{:S(2)}) copy-start(f32[8]{0:T(128)} %get-tuple-element.39) | copy-start | bytes 100
  118.7 5.8 %collective-permute-start.4 = (f32[5,64,8,3]{1,2,3,0:T(8,128)S(1)}, f32[5,64,8,3]{1,2,3,0:T(8,128)S(1)}, u32[]{:S(2)}, u32[]{:S(2)}) collective-permute-start(f32[5,64,8,3]{1,2,3,0:T(8,128)S(1)} %copy.22), channel_id=1, source_target_pairs={{32,0},{64,32},{96,64},{33,1},{65,33},{97,65},{34,2},{66,34},{98,6... | collective-permute-start | bytes 92168 | tf_op jit(solution)/shard_map/ppermute | solution.py:28
  120.5 5.6 %collective-permute-start.5 = (f32[5,64,8,3]{1,2,3,0:T(8,128)S(1)}, f32[5,64,8,3]{1,2,3,0:T(8,128)S(1)}, u32[]{:S(2)}, u32[]{:S(2)}) collective-permute-start(f32[5,64,8,3]{1,2,3,0:T(8,128)S(1)} %copy.24), channel_id=1, source_target_pairs={{0,32},{32,64},{64,96},{1,33},{33,65},{65,97},{2,34},{34,66},{66,9... | collective-permute-start | bytes 92168 | tf_op jit(solution)/shard_map/ppermute | solution.py:26
  181.4 17.9 %collective-permute-start.6 = (f32[5,64,3,128]{3,1,2,0:T(8,128)S(1)}, f32[5,64,3,128]{3,1,2,0:T(8,128)S(1)}, u32[]{:S(2)}, u32[]{:S(2)}) collective-permute-start(f32[5,64,3,128]{3,1,2,0:T(8,128)S(1)} %copy.26), channel_id=1, source_target_pairs={{1,0},{2,1},{3,2},{4,3},{5,4},{6,5},{7,6},{8,7},{9,8},{10,9},{11,1... | collective-permute-start | bytes 1474568 | tf_op jit(solution)/shard_map/ppermute | solution.py:28
  197.8 5.8 %collective-permute-start.7 = (f32[5,64,3,128]{3,1,2,0:T(8,128)S(1)}, f32[5,64,3,128]{3,1,2,0:T(8,128)S(1)}, u32[]{:S(2)}, u32[]{:S(2)}) collective-permute-start(f32[5,64,3,128]{3,1,2,0:T(8,128)S(1)} %copy.28), channel_id=1, source_target_pairs={{0,1},{1,2},{2,3},{3,4},{4,5},{5,6},{6,7},{7,8},{8,9},{9,10},{10,1... | collective-permute-start | bytes 1474568 | tf_op jit(solution)/shard_map/ppermute | solution.py:26
  208.2 3.2 copy-start.16
  208.2 3.2 copy-start.17
  209.0 240.4 %all-reduce.3.cloned.1.call-start = ((), (), s32[]{:S(2)}) async-start(), calls=%async_computation.2 | async-start | bytes 524288
  286.0 164.7 %copy-start.11 = (f32[5,64,8,128]{3,2,1,0:T(8,128)}, f32[5,64,8,128]{3,2,1,0:T(8,128)S(1)}, u32[]{:S(2)}) copy-start(f32[5,64,8,128]{3,2,1,0:T(8,128)S(1)} %fusion.17) | copy-start | bytes 3932164
  (10 other events, 21.5 us)
Sparse Core Ops, SparseCore 0:
  27.2 63.5 all-gather.6
  209.2 59.0 all-gather.8
  308.8 140.6 all-reduce.2
where the time goes:
time: 464 us; the launch traced here: 457 us
  waiting for transfers between devices  209 us (45%)
  matrix products  108 us (23%)
  other arithmetic  44.7 us (10%)
  local copies, waits for them, and re-layouts  30.9 us (7%)
  starting transfers between devices  30.1 us (6%)
  blocking collectives  19.1 us (4%)
  between operations  14.7 us (3%)
    unnamed x4, waiting for transfers between devices  141 us
    all_gather x2, waiting for transfers between devices, cycle_line(): piece = lax.all_gather(moments, 'azim', axis=0, tiled=True)  56.8 us
    dot_general x2, matrix products, open_line(): jnp.einsum('vraj,j->vra', rhs, signed_power(base, offsets), precision=HIG...  35.4 us
    dot_general x2, matrix products, open_line(): jnp.einsum('vraj,j->vra', rhs, signed_power(base, width_here - 1 - offset...  34.6 us
    scatter-add x1, other arithmetic, per_device(): jax.ops.segment_sum(values, bucket, num_segments=OBSERVERS * TIME_BINS)  22.6 us
    ppermute x4, starting transfers between devices, padded(): lax.ppermute(head, axis, [((i + 1) % count, i) for i in range(ends)])  20.4 us
    all_gather x2, blocking collectives, open_line(): piece = lax.all_gather(moments, 'axial', axis=0, tiled=True)  19.1 us
    dot_general x2, matrix products, cycle_line(): last_sum = jnp.einsum('k,kvrx->vrx', w_last, piece[:, 1], precision=HIGHEST)  11.2 us
  transfers between devices with their start and end apart: 11, of which 5 were waited for; matrix products, arithmetic and copies ran while one was open for 13% of the time, Pallas kernels for 0%

commit v1 on v0

--- a/solution.py
+++ b/solution.py
@@ -142,7 +142,14 @@
     )
     last_moment = jnp.einsum("vrjx,j->vrx", rhs, signed_power(base, offsets), precision=HIGHEST)
     moments = jnp.stack([first_moment, last_moment])[None]
-    piece = lax.all_gather(moments, "azim", axis=0, tiled=True)
+    count_all = lax.psum(1, axis_name="azim")
+    piece = lax.all_to_all(
+        jnp.tile(moments, [count_all if p == 0 else 1 for p in range(moments.ndim)]),
+        axis_name="azim",
+        concat_axis=0,
+        tiled=True,
+        split_axis=0,
+    )
     others = jnp.arange(piece.shape[0], dtype=jnp.int32)
     shift = (device_pos - others) % group_size
     w_first = jnp.where(

time: 464 us -> 620 us (1.34)
  waiting for transfers between devices: 209 us -> 334 us
  starting transfers between devices: 30.1 us -> 50.7 us
  local copies, waits for them, and re-layouts: 30.9 us -> 41.3 us
    all_to_all x0 -> x2, waiting for transfers between devices: none -> 177 us  [cycle_line(): lax.all_to_all(jnp.tile(moments, [count_all if p == 0 else 1 for p in ran...]
    all_gather x2 -> x0, waiting for transfers between devices: 56.8 us -> none  [cycle_line(): piece = lax.all_gather(moments, 'azim', axis=0, tiled=True)]
    all_to_all x0 -> x2, starting transfers between devices: none -> 24.7 us  [cycle_line(): lax.all_to_all(jnp.tile(moments, [count_all if p == 0 else 1 for p in ran...]
    another operation x0 -> x2, local copies, waits for them, and re-layouts: none -> 10.4 us  [cycle_line(): jnp.tile(moments, [count_all if p == 0 else 1 for p in range(moments.ndim)])]
    unnamed x4 -> x2, waiting for transfers between devices: 141 us -> 145 us
  transfers between devices with their start and end apart: 11 -> 11, of which waited for: 5 -> 6; matrix products, arithmetic and copies ran while one was open for 13% -> 10% of each run, Pallas kernels for 0% -> 0%
where the time goes in v1:
time: 620 us; the launch traced here: 613 us
  waiting for transfers between devices  334 us (54%)
  matrix products  108 us (17%)
  starting transfers between devices  50.7 us (8%)
  other arithmetic  42.6 us (7%)
  local copies, waits for them, and re-layouts  41.3 us (7%)
  blocking collectives  20.5 us (3%)
  between operations  15 us (2%)
    all_to_all x2, waiting for transfers between devices, cycle_line(): lax.all_to_all(jnp.tile(moments, [count_all if p == 0 else 1 for p in ran...  177 us
    unnamed x2, waiting for transfers between devices  145 us
    dot_general x2, matrix products, open_line(): jnp.einsum('vraj,j->vra', rhs, signed_power(base, offsets), precision=HIG...  35.4 us
    dot_general x2, matrix products, open_line(): jnp.einsum('vraj,j->vra', rhs, signed_power(base, width_here - 1 - offset...  34.6 us
    all_to_all x2, starting transfers between devices, cycle_line(): lax.all_to_all(jnp.tile(moments, [count_all if p == 0 else 1 for p in ran...  24.7 us
    scatter-add x1, other arithmetic, per_device(): jax.ops.segment_sum(values, bucket, num_segments=OBSERVERS * TIME_BINS)  22.6 us
    all_gather x2, blocking collectives, open_line(): piece = lax.all_gather(moments, 'axial', axis=0, tiled=True)  20.5 us
    ppermute x4, starting transfers between devices, padded(): lax.ppermute(head, axis, [((i + 1) % count, i) for i in range(ends)])  16.4 us
  transfers between devices with their start and end apart: 11, of which 6 were waited for; matrix products, arithmetic and copies ran while one was open for 10% of the time, Pallas kernels for 0%

profile of v1, /device:TPU:1, one launch (start us, length us, event | category | flops | bytes accessed | tf_op | source)
XLA Modules:
  0.0 612.8 jit_solution(8884503430977676030)
XLA Ops:
  14.9 6.4 %collective-permute-done.2 = f32[5,64,3,128]{3,1,2,0:T(8,128)S(1)} collective-permute-done((f32[5,64,3,128]{3,1,2,0:T(8,128)S(1)}, f32[5,64,3,128]{3,1,2,0:T(8,128)S(1)}, u32[]{:S(2)}, u32[]{:S(2)}) %collective-permute-start.2) | collective-permute-done | bytes 491552 | tf_op jit(solution)/shard_map/ppermute | solution.py:28
  25.6 5.2 tile.4
  30.8 14.2 %all-to-all-start = ((f32[32,2,5,64,128]{4,3,2,1,0:T(8,128)}), f32[32,2,5,64,128]{4,3,2,1,0:T(8,128)}, u32[]{:S(2)}, u32[]{:S(2)}) async-start(f32[32,2,5,64,128]{4,3,2,1,0:T(8,128)} %tile.4), calls=%async_computation | async-start | bytes 20971520 | tf_op jit(solution)/shard_map/all_to_all | solution.py:146
  60.5 5.6 fusion.30
  66.1 17.3 %fusion.215 = f32[1,5,64,8]{3,0,2,1:T(1,128)S(1)} fusion(f32[5,64,8,128]{3,2,1,0:T(8,128)S(1)} %fusion.30), kind=kOutput, calls=%fused_computation.350 | convolution fusion | flops 3934336 | bytes 1320960 | tf_op jit(solution)/shard_map/vraj,j->vra/dot_general | solution.py:102
  83.6 17.7 %fusion.213 = f32[1,5,64,8]{3,0,2,1:T(1,128)S(1)} fusion(f32[5,64,8,128]{3,2,1,0:T(8,128)S(1)} %fusion.30), kind=kOutput, calls=%fused_computation.348 | convolution fusion | flops 3933568 | bytes 1320960 | tf_op jit(solution)/shard_map/vraj,j->vra/dot_general | solution.py:105
  101.4 10.7 %all-gather = f32[8,5,64,8]{2,3,1,0:T(8,128)S(1)} all-gather(f32[2,5,64,8]{2,3,1,0:T(8,128)S(1)} %pad_maximum_fusion.10), channel_id=2, replica_groups=mesh['axial'=4,'azim'=32] {'axial'}, dimensions={0}, use_global_device_ids=true | all-gather | bytes 102400 | tf_op jit(solution)/shard_map/all_gather | solution.py:107
  115.9 54.4 %all-to-all-done = f32[32,2,5,64,128]{4,3,2,1,0:T(8,128)} async-done(((f32[32,2,5,64,128]{4,3,2,1,0:T(8,128)}), f32[32,2,5,64,128]{4,3,2,1,0:T(8,128)}, u32[]{:S(2)}, u32[]{:S(2)}) %all-to-all-start) | async-done | bytes 10485792 | tf_op jit(solution)/shard_map/all_to_all | solution.py:146
  170.3 5.2 slice_bitcast_fusion.3
  175.5 5.4 fusion.6
  181.0 5.6 fusion.4
  200.6 6.2 %fusion.47 = f32[5,64,8,128]{3,2,1,0:T(8,128)S(1)} fusion(f32[5,64,8,3]{3,2,1,0:T(8,128)} %copy.25, f32[5,64,8,128]{3,2,1,0:T(8,128)S(1)} %fusion.21, f32[5,64,8,3]{3,2,1,0:T(8,128)} %copy.23), kind=kLoop, calls=%fused_computation.81 | loop fusion | flops 5242880 | bytes 2682880 | tf_op jit(solution)/shard_map/add | solution.py:69
  206.9 17.3 %fusion.204 = f32[1,5,64,8]{3,0,2,1:T(1,128)S(1)} fusion(f32[5,64,8,128]{3,2,1,0:T(8,128)S(1)} %fusion.47), kind=kOutput, calls=%fused_computation.339 | convolution fusion | flops 3934336 | bytes 1320960 | tf_op jit(solution)/shard_map/vraj,j->vra/dot_general | solution.py:102
  224.1 17.7 %fusion.202 = f32[1,5,64,8]{3,0,2,1:T(1,128)S(1)} fusion(f32[5,64,8,128]{3,2,1,0:T(8,128)S(1)} %fusion.47), kind=kOutput, calls=%fused_computation.337 | convolution fusion | flops 3933568 | bytes 1320960 | tf_op jit(solution)/shard_map/vraj,j->vra/dot_general | solution.py:105
  242.1 9.7 %all-gather.1 = f32[8,5,64,8]{2,3,1,0:T(8,128)S(1)} all-gather(f32[2,5,64,8]{2,3,1,0:T(8,128)S(1)} %pad_maximum_fusion.11), channel_id=3, replica_groups=mesh['axial'=4,'azim'=32] {'axial'}, dimensions={0}, use_global_device_ids=true | all-gather | bytes 102400 | tf_op jit(solution)/shard_map/all_gather | solution.py:107
  255.0 12.3 %collective-permute-start.6 = (f32[5,64,3,128]{3,1,2,0:T(8,128)S(1)}, f32[5,64,3,128]{3,1,2,0:T(8,128)S(1)}, u32[]{:S(2)}, u32[]{:S(2)}) collective-permute-start(f32[5,64,3,128]{3,1,2,0:T(8,128)S(1)} %copy.26), channel_id=1, source_target_pairs={{1,0},{2,1},{3,2},{4,3},{5,4},{6,5},{7,6},{8,7},{9,8},{10,9},{11,1... | collective-permute-start | bytes 1474568 | tf_op jit(solution)/shard_map/ppermute | solution.py:28
  277.8 5.2 tile.5
  283.0 10.5 %all-to-all-start.1 = ((f32[32,2,5,64,128]{4,3,2,1,0:T(8,128)}), f32[32,2,5,64,128]{4,3,2,1,0:T(8,128)}, u32[]{:S(2)}, u32[]{:S(2)}) async-start(f32[32,2,5,64,128]{4,3,2,1,0:T(8,128)} %tile.5), calls=%async_computation.1 | async-start | bytes 20971520 | tf_op jit(solution)/shard_map/all_to_all | solution.py:146
  295.9 122.8 %all-to-all-done.1 = f32[32,2,5,64,128]{4,3,2,1,0:T(8,128)} async-done(((f32[32,2,5,64,128]{4,3,2,1,0:T(8,128)}), f32[32,2,5,64,128]{4,3,2,1,0:T(8,128)}, u32[]{:S(2)}, u32[]{:S(2)}) %all-to-all-start.1) | async-done | bytes 10485792 | tf_op jit(solution)/shard_map/all_to_all | solution.py:146
  418.8 5.2 slice_bitcast_fusion.1
  424.0 5.4 fusion.2
  429.4 5.6 fusion
  436.5 22.6 %scatter_custom_fusion = f32[65536]{0:T(1024)} fusion(s32[4096]{0:T(1024)S(1)} %add_bitcast_fusion, f32[4096]{0:T(1024)S(1)} %bitcast_multiply_fusion.21, f32[]{:T(128)} %constant.254.clone.1), kind=kCustom, calls=%fused_computation.160 | custom fusion | flops 4096 | bytes 262148 | tf_op jit(solution)/shard_map/scatter-add | solution.py:202
  459.1 145.3 %all-reduce.3.cloned.1.call-done = f32[512,128]{1,0:T(8,128)} async-done(((f32[512,128]{1,0:T(8,128)}), f32[512,128]{1,0:T(8,128)}) %all-reduce.3.cloned.1.call-update) | async-done | bytes 262160
  (130 shorter events, 64.2 us)
Async XLA Ops:
  7.2 286.4 %copy-start = (f32[256]{0:T(256)S(1)}, f32[256]{0:T(256)}, u32[]{:S(2)}) copy-start(f32[256]{0:T(256)} %param.23) | copy-start | bytes 3076
  11.8 33.2 %copy-start.12 = (f32[64,8,128]{2,1,0:T(8,128)}, f32[64,8,128]{2,1,0:T(8,128)S(1)}, u32[]{:S(2)}) copy-start(f32[64,8,128]{2,1,0:T(8,128)S(1)} %get-tuple-element.3) | copy-start | bytes 786436
  12.0 9.3 %collective-permute-start.2 = (f32[5,64,3,128]{3,1,2,0:T(8,128)S(1)}, f32[5,64,3,128]{3,1,2,0:T(8,128)S(1)}, u32[]{:S(2)}, u32[]{:S(2)}) collective-permute-start(f32[5,64,3,128]{3,1,2,0:T(8,128)S(1)} %copy.18), channel_id=1, source_target_pairs={{1,0},{2,1},{3,2},{4,3},{5,4},{6,5},{7,6},{8,7},{9,8},{10,9},{11,1... | collective-permute-start | bytes 1474568 | tf_op jit(solution)/shard_map/ppermute | solution.py:28
  13.6 8.1 %collective-permute-start.3 = (f32[5,64,3,128]{3,1,2,0:T(8,128)S(1)}, f32[5,64,3,128]{3,1,2,0:T(8,128)S(1)}, u32[]{:S(2)}, u32[]{:S(2)}) collective-permute-start(f32[5,64,3,128]{3,1,2,0:T(8,128)S(1)} %copy.20), channel_id=1, source_target_pairs={{0,1},{1,2},{2,3},{3,4},{4,5},{5,6},{6,7},{7,8},{8,9},{9,10},{10,1... | collective-permute-start | bytes 1474568 | tf_op jit(solution)/shard_map/ppermute | solution.py:26
  30.8 139.4 %all-to-all-start = ((f32[32,2,5,64,128]{4,3,2,1,0:T(8,128)}), f32[32,2,5,64,128]{4,3,2,1,0:T(8,128)}, u32[]{:S(2)}, u32[]{:S(2)}) async-start(f32[32,2,5,64,128]{4,3,2,1,0:T(8,128)} %tile.4), calls=%async_computation | async-start | bytes 20971520 | tf_op jit(solution)/shard_map/all_to_all | solution.py:146
  48.3 9.1 %collective-permute-start = (f32[5,64,8,3]{1,2,3,0:T(8,128)S(1)}, f32[5,64,8,3]{1,2,3,0:T(8,128)S(1)}, u32[]{:S(2)}, u32[]{:S(2)}) collective-permute-start(f32[5,64,8,3]{1,2,3,0:T(8,128)S(1)} %copy.14), channel_id=1, source_target_pairs={{32,0},{64,32},{96,64},{33,1},{65,33},{97,65},{34,2},{66,34},{98,6... | collective-permute-start | bytes 92168 | tf_op jit(solution)/shard_map/ppermute | solution.py:28
  50.7 8.3 %collective-permute-start.1 = (f32[5,64,8,3]{1,2,3,0:T(8,128)}, f32[5,64,8,3]{1,2,3,0:T(8,128)S(1)}, u32[]{:S(2)}, u32[]{:S(2)}) collective-permute-start(f32[5,64,8,3]{1,2,3,0:T(8,128)} %copy.16), channel_id=1, source_target_pairs={{0,32},{32,64},{64,96},{1,33},{33,65},{65,97},{2,34},{34,66},{66,9... | collective-permute-start | bytes 92168 | tf_op jit(solution)/shard_map/ppermute | solution.py:26
  175.4 11.1 %copy-start.21 = (f32[5,64,8,128]{3,2,1,0:T(8,128)S(1)}, f32[5,64,8,128]{3,2,1,0:T(8,128)}, u32[]{:S(2)}) copy-start(f32[5,64,8,128]{3,2,1,0:T(8,128)} %fusion.19) | copy-start | bytes 3932164
  180.9 5.7 copy-start.3
  180.9 5.7 copy-start.5
  180.9 5.7 copy-start.10
  180.9 5.7 copy-start.13
  180.9 5.7 copy-start.14
  180.9 5.7 copy-start.18
  191.7 5.8 collective-permute-start.4
  193.5 5.6 collective-permute-start.5
  255.0 13.8 %collective-permute-start.6 = (f32[5,64,3,128]{3,1,2,0:T(8,128)S(1)}, f32[5,64,3,128]{3,1,2,0:T(8,128)S(1)}, u32[]{:S(2)}, u32[]{:S(2)}) collective-permute-start(f32[5,64,3,128]{3,1,2,0:T(8,128)S(1)} %copy.26), channel_id=1, source_target_pairs={{1,0},{2,1},{3,2},{4,3},{5,4},{6,5},{7,6},{8,7},{9,8},{10,9},{11,1... | collective-permute-start | bytes 1474568 | tf_op jit(solution)/shard_map/ppermute | solution.py:28
  267.4 5.8 collective-permute-start.7
  283.0 10.6 %copy-start.19 = (s32[4,8,128]{2,1,0:T(8,128)S(1)}, s32[4,8,128]{2,1,0:T(8,128)}, u32[]{:S(2)}) copy-start(s32[4,8,128]{2,1,0:T(8,128)} %param.22) | copy-start | bytes 49156
  283.0 12.9 %copy-start.15 = (s32[4,8,128]{2,1,0:T(8,128)S(1)}, s32[4,8,128]{2,1,0:T(8,128)}, u32[]{:S(2)}) copy-start(s32[4,8,128]{2,1,0:T(8,128)} %param.21) | copy-start | bytes 49156
  283.0 12.9 %copy-start.16 = (s32[4,8,128]{2,1,0:T(8,128)S(1)}, s32[4,8,128]{2,1,0:T(8,128)}, u32[]{:S(2)}) copy-start(s32[4,8,128]{2,1,0:T(8,128)} %param.20) | copy-start | bytes 49156
  283.0 135.8 %all-to-all-start.1 = ((f32[32,2,5,64,128]{4,3,2,1,0:T(8,128)}), f32[32,2,5,64,128]{4,3,2,1,0:T(8,128)}, u32[]{:S(2)}, u32[]{:S(2)}) async-start(f32[32,2,5,64,128]{4,3,2,1,0:T(8,128)} %tile.5), calls=%async_computation.1 | async-start | bytes 20971520 | tf_op jit(solution)/shard_map/all_to_all | solution.py:146
  293.5 310.9 %all-reduce.3.cloned.1.call-start = ((), (), s32[]{:S(2)}) async-start(), calls=%async_computation.2 | async-start | bytes 524288
  436.5 169.2 %copy-start.11 = (f32[5,64,8,128]{3,2,1,0:T(8,128)}, f32[5,64,8,128]{3,2,1,0:T(8,128)S(1)}, u32[]{:S(2)}) copy-start(f32[5,64,8,128]{3,2,1,0:T(8,128)S(1)} %fusion.17) | copy-start | bytes 3932164
  (9 other events, 20.7 us)
Sparse Core Ops, SparseCore 0:
  459.3 145.1 all-reduce.2
